TPU v7x, 512 devices: a whole 4x4x16 slice. The times are simulated.
512 devices in a mesh: rows: 64 (over x_lo, z, core), blk: 8 (over x_hi, y).
Axes of the slice: x: 4 (x_hi: 2, x_lo: 2; x = x_hi * 2 + x_lo), y: 4, z: 16, core: 2. Of those that a mesh axis runs over, the one named last changes fastest.
Arguments:
- cov_blocks: bfloat16 [1024, 40, 128, 128], P(('rows', 'blk')), may hold values from -24 to 24
- col_index: int32 [1024, 40], P(('rows', 'blk')), may hold values from 0 to 1023, as said below
- block_count: int32 [1024], P(('rows', 'blk')), may hold values from 2 to 40, as said below
- probes: bfloat16 [131072, 512], P(('rows', 'blk')), may hold values from -60 to 60
Outputs:
- basis: float32 [131072, 512], P(('rows', 'blk'))
Inputs may be any that keep to these rules, and one draw needn't show every extreme that they name: `col_index`: the live slots of block row i name distinct column blocks of zone i // 16 or of an adjacent zone; rows of the first and last zone have at most 32 live slots; every entry of a row is distinct. `block_count`: some block row uses all 40 slots in every draw.
All inputs are finite; a program needn't handle non-finite values.
Results may differ from a plain program's by a relative error of at most 0.0003.
Values may be sent and summed in bfloat16 or wider, within the bound.
A program may use at most 64 MiB of HBM per device.

v0:
```python
import jax
import jax.numpy as jnp
from jax import lax
from jax.sharding import PartitionSpec as P


def extended(x, sides, width):
    for axis, dim in sides:
        devices, length = (lax.axis_size(axis), x.shape[dim])
        up = [(i, (i + 1) % devices) for i in range(devices - 1)]
        down = [(j, i) for i, j in up]
        last = lax.slice_in_dim(x, length - width, length, axis=dim)
        first = lax.slice_in_dim(x, 0, width, axis=dim)
        before = lax.ppermute(last, axis, up)
        after = lax.ppermute(first, axis, down)
        x = jnp.concatenate([before, x, after], axis=dim)
    return x


def local(cov_blocks, col_index, block_count, probes):
    rows_here, slots, block, _ = cov_blocks.shape
    tile_rows = probes.shape[0]
    probe_cols = probes.shape[1]
    zone_blocks = rows_here * lax.axis_size("blk")
    zone_number = lax.axis_index("rows")
    relative = col_index - (zone_number - 1) * zone_blocks
    window_blocks = 3 * zone_blocks
    inside = (relative >= 0) & (relative < window_blocks)
    slot_ids = lax.broadcasted_iota(jnp.int32, (rows_here, slots), 1)
    live_mask = inside & (slot_ids < block_count[:, None])
    column_ids = jnp.arange(window_blocks, dtype=jnp.int32)
    hits = (relative[:, :, None] == column_ids[None, None, :]) & live_mask[:, :, None]
    selector = hits.astype(jnp.bfloat16)
    window_matrix = jnp.einsum(
        "lsp,lsac->lapc", selector, cov_blocks, preferred_element_type=jnp.float32
    )
    window_matrix = window_matrix.astype(jnp.bfloat16).reshape(
        rows_here * block, window_blocks * block
    )

    def add_columns(running, shard_rows, first_row):
        length = shard_rows.shape[0]
        columns = lax.dynamic_slice_in_dim(window_matrix, first_row, length, 1)
        return running + jnp.dot(columns, shard_rows, preferred_element_type=jnp.float32)

    zeros_out = jnp.zeros((tile_rows, probe_cols), jnp.float32)
    own_zone = lax.all_gather(probes, "blk", axis=0, tiled=True)
    zone_length = own_zone.shape[0]
    images = add_columns(zeros_out, own_zone, zone_length)
    near_zones = extended(own_zone, (("rows", 0),), zone_length)
    images = add_columns(images, lax.slice_in_dim(near_zones, 0, zone_length, axis=0), 0)
    images = add_columns(
        images,
        lax.slice_in_dim(near_zones, 2 * zone_length, 3 * zone_length, axis=0),
        2 * zone_length,
    )
    gram_local = lax.dot_general(
        images,
        images,
        (((0,), (0,)), ((), ())),
        precision=lax.Precision.HIGHEST,
        preferred_element_type=jnp.float32,
    )
    gram_total = lax.psum(gram_local, ("rows", "blk"))
    point_count = tile_rows * lax.axis_size("rows") * lax.axis_size("blk")
    gram_matrix = gram_total / point_count
    factor = jnp.linalg.cholesky(gram_matrix)
    return lax.linalg.triangular_solve(
        factor, images, left_side=False, lower=True, transpose_a=True
    )


def solution(mesh):
    return jax.shard_map(
        local,
        mesh=mesh,
        in_specs=(
            P(("rows", "blk"), None, None, None),
            P(("rows", "blk"), None),
            P(("rows", "blk")),
            P(("rows", "blk"), None),
        ),
        out_specs=P(("rows", "blk"), None),
        check_vma=False,
    )
```

profile of v0, /device:TPU:1, one launch (start us, length us, event | category | flops | bytes accessed | tf_op | source)
XLA Modules:
  0.0 755.8 jit_solution(5842420707224924274)
XLA Ops:
  6.5 0.7 all-gather.2.cloned.1.call-update
  7.3 77.5 %all-gather.2.cloned.1.call-done = bf16[2048,512]{1,0:T(8,128)(2,1)} async-done(((bf16[256,512]{1,0:T(8,128)(2,1)}), bf16[2048,512]{1,0:T(8,128)(2,1)}) %all-gather.2.cloned.1.call-update) | async-done | bytes 2097168 | tf_op jit(solution)/shard_map/all_gather | solution.py:47
  84.8 4.1 collective-permute-start
  89.0 1.9 collective-permute-start.1
  90.9 0.8 compare_and_fusion
  91.7 2.7 fusion.2
  94.4 0.8 copy.17
  95.2 0.8 copy-done.2
  96.0 0.7 fusion.7
  96.7 15.6 %collective-permute-done = bf16[2048,512]{1,0:T(8,128)(2,1)} collective-permute-done((bf16[2048,512]{1,0:T(8,128)(2,1)}, bf16[2048,512]{1,0:T(8,128)(2,1)}, u32[]{:S(2)}, u32[]{:S(2)}) %collective-permute-start) | collective-permute-done | bytes 2097184 | tf_op jit(solution)/shard_map/ppermute | solution.py:14
  112.3 2.3 convolution_add_fusion.1
  114.6 2.1 collective-permute-done.1
  116.7 2.3 convolution_add_fusion
  119.0 2.1 fusion.48
  121.1 464.7 %all-reduce.3.cloned.1.call-done = f32[512,512]{0,1:T(8,128)} async-done(((f32[512,512]{0,1:T(8,128)}), f32[512,512]{0,1:T(8,128)}) %all-reduce.3.cloned.1.call-update) | async-done | bytes 1048592 | tf_op jit(solution)/shard_map/psum | solution.py:64
  585.8 2.3 broadcast_multiply_fusion
  588.1 2.6 copy.7
  590.7 1.8 fusion.9
  592.5 1.0 copy-done.1
  593.5 11.7 %cholesky.104 = f32[128,128]{1,0:T(8,128)S(1)} custom-call(f32[128,128]{1,0:T(8,128)S(1)} %cholesky.266), custom_call_target="Cholesky" | custom-call | tf_op jit(solution)/shard_map/jit(cholesky)/cholesky | solution.py:67
  605.2 9.8 %custom-call.30 = f32[1,128,128]{1,2,0:T(8,128)S(1)} custom-call(f32[1,128,128]{2,1,0:T(8,128)S(1)} %get-tuple-element.34), custom_call_target="InvertDiagBlocksLowerTriangular" | custom-call | tf_op jit(solution)/shard_map/jit(cholesky)/cholesky | solution.py:67
  615.1 1.2 cholesky.224
  616.2 2.1 constant_dynamic-update-slice_fusion.3
  618.4 1.3 convolution_subtract_fusion
  619.6 11.7 %cholesky.217 = f32[128,128]{1,0:T(8,128)S(1)} custom-call(f32[128,128]{1,0:T(8,128)S(1)} %cholesky.270), custom_call_target="Cholesky" | custom-call | tf_op jit(solution)/shard_map/jit(cholesky)/cholesky | solution.py:67
  631.4 0.6 select_reduce_fusion.2
  632.0 9.8 %custom-call.31 = f32[1,128,128]{1,2,0:T(8,128)S(1)} custom-call(f32[1,128,128]{2,1,0:T(8,128)S(1)} %get-tuple-element.31), custom_call_target="InvertDiagBlocksLowerTriangular" | custom-call | tf_op jit(solution)/shard_map/jit(cholesky)/cholesky | solution.py:67
  641.8 0.9 convolution_dynamic-update-slice_fusion
  642.8 1.4 convolution_subtract_fusion.1
  644.2 11.7 %cholesky.238 = f32[128,128]{1,0:T(8,128)S(1)} custom-call(f32[128,128]{1,0:T(8,128)S(1)} %cholesky.275), custom_call_target="Cholesky" | custom-call | tf_op jit(solution)/shard_map/jit(cholesky)/cholesky | solution.py:67
  656.6 0.6 compare_reduce_fusion.1
  657.2 10.0 %custom-call.32 = f32[1,128,128]{1,2,0:T(8,128)S(1)} custom-call(f32[1,128,128]{2,1,0:T(8,128)S(1)} %get-tuple-element.28), custom_call_target="InvertDiagBlocksLowerTriangular" | custom-call | tf_op jit(solution)/shard_map/jit(cholesky)/cholesky | solution.py:67
  667.2 0.8 convolution_dynamic-update-slice_fusion.1
  668.0 1.4 convolution_subtract_fusion.2
  669.5 11.7 %cholesky.255 = f32[128,128]{1,0:T(8,128)S(1)} custom-call(f32[128,128]{1,0:T(8,128)S(1)} %convolution_subtract_fusion.2), custom_call_target="Cholesky" | custom-call | tf_op jit(solution)/shard_map/jit(cholesky)/cholesky | solution.py:67
  681.2 0.7 select_reduce_fusion
  681.8 0.7 compare_reduce_fusion
  685.5 2.4 select_select_fusion
  687.9 14.1 %while.1 = (s32[]{:T(128)}, f32[512,512]{1,0:T(8,128)}, s32[4,2]{0,1:T(2,128)S(1)}, f32[4,128,128]{2,1,0:T(8,128)}, s32[]{:T(128)}) while((s32[]{:T(128)}, f32[512,512]{1,0:T(8,128)}, s32[4,2]{0,1:T(2,128)S(1)}, f32[4,128,128]{2,1,0:T(8,128)}, s32[]{:T(128)}) %tuple.28), condition=%wide.while_cond, body=%wide.while_body.sunk | while | flops 2 | bytes 132705 | solution.py:68
  688.6 2.9 bitcast_dynamic-update-slice_fusion.2
  692.1 2.9 bitcast_dynamic-update-slice_fusion.2
  695.7 2.9 bitcast_dynamic-update-slice_fusion.2
  699.2 2.8 bitcast_dynamic-update-slice_fusion.2
  702.0 40.1 %custom-call.33 = f32[4,128,128]{1,2,0:T(8,128)S(1)} custom-call(f32[4,128,128]{2,1,0:T(8,128)} %get-tuple-element.12), custom_call_target="InvertDiagBlocksLowerTriangular" | custom-call | tf_op jit(solution)/shard_map/triangular_solve | solution.py:68
  742.5 1.2 fusion.33
  744.0 1.5 fusion.17
  745.9 1.7 fusion.10
  748.0 1.0 copy.8
  (29 shorter events, 5.4 us)
Async XLA Ops:
  6.5 85.2 %copy-start = (bf16[2,40,128,128]{3,2,1,0:T(8,128)(2,1)S(1)}, bf16[2,40,128,128]{3,2,1,0:T(8,128)(2,1)}, u32[]{:S(2)}) copy-start(bf16[2,40,128,128]{3,2,1,0:T(8,128)(2,1)} %param.4) | copy-start | bytes 7864324
  6.5 78.3 %all-gather.2.cloned.1.call-start = ((), (), s32[]{:S(2)}) async-start(), calls=%async_computation | async-start | bytes 2359296 | tf_op jit(solution)/shard_map/all_gather | solution.py:47
  7.3 578.6 %all-reduce.3.cloned.1.call-start = ((), (), s32[]{:S(2)}) async-start(), calls=%async_computation.1 | async-start | bytes 2097152 | tf_op jit(solution)/shard_map/psum | solution.py:64
  84.8 27.4 %collective-permute-start = (bf16[2048,512]{1,0:T(8,128)(2,1)}, bf16[2048,512]{1,0:T(8,128)(2,1)}, u32[]{:S(2)}, u32[]{:S(2)}) collective-permute-start(bf16[2048,512]{1,0:T(8,128)(2,1)} %all-gather.2.cloned.1.call-done), channel_id=1, source_target_pairs={{0,8},{8,16},{16,24},{24,32},{32,40},{40,48},{48,56},{56,64},{64,7... | collective-permute-start | bytes 6291464 | tf_op jit(solution)/shard_map/ppermute | solution.py:14
  89.0 27.7 %collective-permute-start.1 = (bf16[2048,512]{1,0:T(8,128)(2,1)}, bf16[2048,512]{1,0:T(8,128)(2,1)}, u32[]{:S(2)}, u32[]{:S(2)}) collective-permute-start(bf16[2048,512]{1,0:T(8,128)(2,1)} %all-gather.2.cloned.1.call-done), channel_id=1, source_target_pairs={{8,0},{16,8},{24,16},{32,24},{40,32},{48,40},{56,48},{64,56},{72,6... | collective-permute-start | bytes 6291464 | tf_op jit(solution)/shard_map/ppermute | solution.py:15
  94.4 1.6 copy-start.2
  592.5 1.0 copy-start.1
Sparse Core Ops, SparseCore 0:
  10.6 74.2 all-gather.1
  121.2 464.5 all-reduce.2
where the time goes:
time: 757 us; the launch traced here: 756 us
  waiting for transfers between devices  561 us (74%)
  other arithmetic  128 us (17%)
  matrix products  23.8 us (3%)
  local copies, waits for them, and re-layouts  21.5 us (3%)
  between operations  16 us (2%)
    psum x1, waiting for transfers between devices, local(): gram_total = lax.psum(gram_local, ('rows', 'blk'))  465 us
    another operation x14, other arithmetic, local(): factor = jnp.linalg.cholesky(gram_matrix)  80.4 us
    all_gather x1, waiting for transfers between devices, local(): own_zone = lax.all_gather(probes, 'blk', axis=0, tiled=True)  77.5 us
    another operation x4, other arithmetic, local(): lax.linalg.triangular_solve(factor, images, left_side=False, lower=True,...  42.5 us
    ppermute x1, waiting for transfers between devices, extended(): before = lax.ppermute(last, axis, up)  15.6 us
  transfers between devices with their start and end apart: 4, of which 4 were waited for; matrix products, arithmetic and copies ran while one was open for 1% of the time, Pallas kernels for 0%

commit v1 on v0

--- a/solution.py
+++ b/solution.py
@@ -61,7 +61,7 @@
         precision=lax.Precision.HIGHEST,
         preferred_element_type=jnp.float32,
     )
-    gram_total = lax.psum(gram_local, ("rows", "blk"))
+    gram_total = lax.psum(lax.psum(gram_local, "blk"), "rows")
     point_count = tile_rows * lax.axis_size("rows") * lax.axis_size("blk")
     gram_matrix = gram_total / point_count
     factor = jnp.linalg.cholesky(gram_matrix)

time: 757 us -> 826 us (1.091)
  waiting for transfers between devices: 561 us -> 630 us
    psum x1 -> x2, waiting for transfers between devices: 465 us -> 534 us  [local(): gram_total = lax.psum(lax.psum(gram_local, 'blk'), 'rows')]
  transfers between devices with their start and end apart: 4 -> 5, of which waited for: 4 -> 5; matrix products, arithmetic and copies ran while one was open for 1% -> 1% of each run, Pallas kernels for 0% -> 0%
where the time goes in v1:
time: 826 us
  waiting for transfers between devices  630 us (76%)
  other arithmetic  128 us (15%)
  matrix products  23.6 us (3%)
  local copies, waits for them, and re-layouts  21.5 us (3%)
  between operations  15.7 us (2%)
    psum x2, waiting for transfers between devices, local(): gram_total = lax.psum(lax.psum(gram_local, 'blk'), 'rows')  534 us
    another operation x14, other arithmetic, local(): factor = jnp.linalg.cholesky(gram_matrix)  80.6 us
    all_gather x1, waiting for transfers between devices, local(): own_zone = lax.all_gather(probes, 'blk', axis=0, tiled=True)  77.5 us
    another operation x4, other arithmetic, local(): lax.linalg.triangular_solve(factor, images, left_side=False, lower=True,...  42.5 us
  transfers between devices with their start and end apart: 5, of which 5 were waited for; matrix products, arithmetic and copies ran while one was open for 1% of the time, Pallas kernels for 0%

profile of v1, /device:TPU:1, one launch (start us, length us, event | category | flops | bytes accessed | tf_op | source)
XLA Modules:
  0.0 825.5 jit_solution(3335916607384475046)
XLA Ops:
  6.5 0.7 all-gather.2.cloned.1.call-update
  7.3 77.5 %all-gather.2.cloned.1.call-done = bf16[2048,512]{1,0:T(8,128)(2,1)} async-done(((bf16[256,512]{1,0:T(8,128)(2,1)}), bf16[2048,512]{1,0:T(8,128)(2,1)}) %all-gather.2.cloned.1.call-update) | async-done | bytes 2097168 | tf_op jit(solution)/shard_map/all_gather | solution.py:47
  84.8 4.1 collective-permute-start
  89.0 1.9 collective-permute-start.1
  90.9 0.8 compare_and_fusion
  91.7 2.7 fusion.2
  94.4 0.8 copy.17
  95.2 0.8 copy-done.2
  96.0 0.7 fusion.7
  96.7 15.6 %collective-permute-done = bf16[2048,512]{1,0:T(8,128)(2,1)} collective-permute-done((bf16[2048,512]{1,0:T(8,128)(2,1)}, bf16[2048,512]{1,0:T(8,128)(2,1)}, u32[]{:S(2)}, u32[]{:S(2)}) %collective-permute-start) | collective-permute-done | bytes 2097184 | tf_op jit(solution)/shard_map/ppermute | solution.py:14
  112.3 2.3 convolution_add_fusion.1
  114.6 2.1 collective-permute-done.1
  116.7 2.3 convolution_add_fusion
  119.0 2.0 fusion.48
  121.3 96.0 %all-reduce.4.cloned.1.call-done = f32[512,512]{0,1:T(8,128)} async-done(((f32[512,512]{0,1:T(8,128)}), f32[512,512]{0,1:T(8,128)}) %all-reduce.4.cloned.1.call-update) | async-done | bytes 1048592 | tf_op jit(solution)/shard_map/psum | solution.py:64
  217.3 438.4 %all-reduce.6.cloned.1.call-done = f32[512,512]{0,1:T(8,128)} async-done(((f32[512,512]{0,1:T(8,128)}), f32[512,512]{0,1:T(8,128)}) %all-reduce.6.cloned.1.call-update) | async-done | bytes 1048592 | tf_op jit(solution)/shard_map/psum | solution.py:64
  655.8 2.3 broadcast_multiply_fusion
  658.1 2.6 copy.7
  660.7 1.8 fusion.9
  662.5 1.0 copy-done.1
  663.5 11.7 %cholesky.104 = f32[128,128]{1,0:T(8,128)S(1)} custom-call(f32[128,128]{1,0:T(8,128)S(1)} %cholesky.266), custom_call_target="Cholesky" | custom-call | tf_op jit(solution)/shard_map/jit(cholesky)/cholesky | solution.py:67
  675.2 9.8 %custom-call.30 = f32[1,128,128]{1,2,0:T(8,128)S(1)} custom-call(f32[1,128,128]{2,1,0:T(8,128)S(1)} %get-tuple-element.34), custom_call_target="InvertDiagBlocksLowerTriangular" | custom-call | tf_op jit(solution)/shard_map/jit(cholesky)/cholesky | solution.py:67
  685.0 1.2 cholesky.224
  686.2 2.0 constant_dynamic-update-slice_fusion.3
  688.2 1.2 convolution_subtract_fusion
  689.4 11.7 %cholesky.217 = f32[128,128]{1,0:T(8,128)S(1)} custom-call(f32[128,128]{1,0:T(8,128)S(1)} %cholesky.270), custom_call_target="Cholesky" | custom-call | tf_op jit(solution)/shard_map/jit(cholesky)/cholesky | solution.py:67
  701.1 0.6 select_reduce_fusion.2
  701.8 10.0 %custom-call.31 = f32[1,128,128]{1,2,0:T(8,128)S(1)} custom-call(f32[1,128,128]{2,1,0:T(8,128)S(1)} %get-tuple-element.31), custom_call_target="InvertDiagBlocksLowerTriangular" | custom-call | tf_op jit(solution)/shard_map/jit(cholesky)/cholesky | solution.py:67
  711.8 0.9 convolution_dynamic-update-slice_fusion
  712.7 1.4 convolution_subtract_fusion.1
  714.2 11.7 %cholesky.238 = f32[128,128]{1,0:T(8,128)S(1)} custom-call(f32[128,128]{1,0:T(8,128)S(1)} %cholesky.275), custom_call_target="Cholesky" | custom-call | tf_op jit(solution)/shard_map/jit(cholesky)/cholesky | solution.py:67
  727.2 9.8 %custom-call.32 = f32[1,128,128]{1,2,0:T(8,128)S(1)} custom-call(f32[1,128,128]{2,1,0:T(8,128)S(1)} %get-tuple-element.28), custom_call_target="InvertDiagBlocksLowerTriangular" | custom-call | tf_op jit(solution)/shard_map/jit(cholesky)/cholesky | solution.py:67
  737.0 0.8 convolution_dynamic-update-slice_fusion.1
  737.8 1.4 convolution_subtract_fusion.2
  739.2 11.7 %cholesky.255 = f32[128,128]{1,0:T(8,128)S(1)} custom-call(f32[128,128]{1,0:T(8,128)S(1)} %convolution_subtract_fusion.2), custom_call_target="Cholesky" | custom-call | tf_op jit(solution)/shard_map/jit(cholesky)/cholesky | solution.py:67
  750.9 0.7 select_reduce_fusion
  751.6 0.9 compare_reduce_fusion
  755.6 2.4 select_select_fusion
  757.9 14.1 %while.1 = (s32[]{:T(128)}, f32[512,512]{1,0:T(8,128)}, s32[4,2]{0,1:T(2,128)S(1)}, f32[4,128,128]{2,1,0:T(8,128)}, s32[]{:T(128)}) while((s32[]{:T(128)}, f32[512,512]{1,0:T(8,128)}, s32[4,2]{0,1:T(2,128)S(1)}, f32[4,128,128]{2,1,0:T(8,128)}, s32[]{:T(128)}) %tuple.28), condition=%wide.while_cond, body=%wide.while_body.sunk | while | flops 2 | bytes 132705 | solution.py:68
  758.6 2.9 bitcast_dynamic-update-slice_fusion.2
  762.1 2.9 bitcast_dynamic-update-slice_fusion.2
  765.7 2.9 bitcast_dynamic-update-slice_fusion.2
  769.2 2.8 bitcast_dynamic-update-slice_fusion.2
  772.1 40.1 %custom-call.33 = f32[4,128,128]{1,2,0:T(8,128)S(1)} custom-call(f32[4,128,128]{2,1,0:T(8,128)} %get-tuple-element.12), custom_call_target="InvertDiagBlocksLowerTriangular" | custom-call | tf_op jit(solution)/shard_map/triangular_solve | solution.py:68
  812.5 1.2 fusion.33
  814.1 1.5 fusion.17
  815.9 1.7 fusion.10
  818.0 1.0 copy.8
  (32 shorter events, 6.3 us)
Async XLA Ops:
  6.5 85.2 %copy-start = (bf16[2,40,128,128]{3,2,1,0:T(8,128)(2,1)S(1)}, bf16[2,40,128,128]{3,2,1,0:T(8,128)(2,1)}, u32[]{:S(2)}) copy-start(bf16[2,40,128,128]{3,2,1,0:T(8,128)(2,1)} %param.4) | copy-start | bytes 7864324
  6.5 78.3 %all-gather.2.cloned.1.call-start = ((), (), s32[]{:S(2)}) async-start(), calls=%async_computation | async-start | bytes 2359296 | tf_op jit(solution)/shard_map/all_gather | solution.py:47
  7.3 210.0 %all-reduce.4.cloned.1.call-start = ((), (), s32[]{:S(2)}) async-start(), calls=%async_computation.1 | async-start | bytes 2097152 | tf_op jit(solution)/shard_map/psum | solution.py:64
  84.8 27.4 %collective-permute-start = (bf16[2048,512]{1,0:T(8,128)(2,1)}, bf16[2048,512]{1,0:T(8,128)(2,1)}, u32[]{:S(2)}, u32[]{:S(2)}) collective-permute-start(bf16[2048,512]{1,0:T(8,128)(2,1)} %all-gather.2.cloned.1.call-done), channel_id=1, source_target_pairs={{0,8},{8,16},{16,24},{24,32},{32,40},{40,48},{48,56},{56,64},{64,7... | collective-permute-start | bytes 6291464 | tf_op jit(solution)/shard_map/ppermute | solution.py:14
  89.0 27.7 %collective-permute-start.1 = (bf16[2048,512]{1,0:T(8,128)(2,1)}, bf16[2048,512]{1,0:T(8,128)(2,1)}, u32[]{:S(2)}, u32[]{:S(2)}) collective-permute-start(bf16[2048,512]{1,0:T(8,128)(2,1)} %all-gather.2.cloned.1.call-done), channel_id=1, source_target_pairs={{8,0},{16,8},{24,16},{32,24},{40,32},{48,40},{56,48},{64,56},{72,6... | collective-permute-start | bytes 6291464 | tf_op jit(solution)/shard_map/ppermute | solution.py:15
  94.4 1.6 copy-start.2
  121.0 534.8 %all-reduce.6.cloned.1.call-start = ((), (), s32[]{:S(2)}) async-start(), calls=%async_computation.2 | async-start | bytes 2097152 | tf_op jit(solution)/shard_map/psum | solution.py:64
  662.5 1.0 copy-start.1
Sparse Core Ops, SparseCore 0:
  10.6 74.2 all-gather.1
  121.1 96.1 all-reduce.3
  220.2 435.5 all-reduce.5
